TPU v7x, 32 devices: a whole 2x2x4 slice. The times are simulated.
32 devices in a mesh: tab: 8 (over z, x), blk: 4 (over y, core).
Axes of the slice: x: 2, y: 2, z: 4, core: 2. Of those that a mesh axis runs over, the one named last changes fastest.
Arguments:
- tables: bfloat16 [64, 512, 768], P('tab', 'blk'), may hold values from -6 to 6
- lengths: int32 [64], P('tab'), may hold values from 60 to 512, as said below
- cotangent: bfloat16 [64, 512, 768], P('tab', 'blk'), may hold values from -6 to 6
- step_count: int32 [1], replicated, may hold values from 2 to 20
- w_qkv: float32 [768, 2304], P('tab'), may hold values from -0.21875 to 0.21875
- w_out: float32 [768, 768], P('tab'), may hold values from -3.5 to 3.5
- w_up: float32 [768, 3072], P('tab'), may hold values from -0.21875 to 0.21875
- w_down: float32 [3072, 768], P('tab'), may hold values from -0.109375 to 0.109375
- vectors: float32 [768, 12], P('tab')
- first_qkv: float32 [768, 2304], P('tab'), may hold values from -128 to 128
- first_out: float32 [768, 768], P('tab'), may hold values from -12 to 12
- first_up: float32 [768, 3072], P('tab'), may hold values from -80 to 80
- first_down: float32 [3072, 768], P('tab'), may hold values from -64 to 64
- first_vec: float32 [768, 12], P('tab'), may hold values from -128 to 128
- second_qkv: float32 [768, 2304], P('tab'), may hold values from 16.384 to 262.144
- second_out: float32 [768, 768], P('tab'), may hold values from 0.16384 to 2.62144
- second_up: float32 [768, 3072], P('tab'), may hold values from 8.192 to 131.072
- second_down: float32 [3072, 768], P('tab'), may hold values from 5.89824 to 95.0272
- second_vec: float32 [768, 12], P('tab'), may hold values from 16.384 to 262.144
Outputs:
- output: bfloat16 [64, 512, 768], P('tab', 'blk')
- grad_input: float32 [64, 512, 768], P('tab', 'blk')
- moment_qkv: float32 [768, 2304], P('tab')
- square_qkv: float32 [768, 2304], P('tab')
- master_qkv: float32 [768, 2304], P('tab')
- copy_qkv: bfloat16 [768, 2304], P('tab')
- moment_out: float32 [768, 768], P('tab')
- square_out: float32 [768, 768], P('tab')
- master_out: float32 [768, 768], P('tab')
- copy_out: bfloat16 [768, 768], P('tab')
- moment_up: float32 [768, 3072], P('tab')
- square_up: float32 [768, 3072], P('tab')
- master_up: float32 [768, 3072], P('tab')
- copy_up: bfloat16 [768, 3072], P('tab')
- moment_down: float32 [3072, 768], P('tab')
- square_down: float32 [3072, 768], P('tab')
- master_down: float32 [3072, 768], P('tab')
- copy_down: bfloat16 [3072, 768], P('tab')
- moment_vec: float32 [768, 12], P('tab')
- square_vec: float32 [768, 12], P('tab')
- master_vec: float32 [768, 12], P('tab')
- copy_vec: bfloat16 [768, 12], P('tab')
Inputs may be any that keep to these rules, and one draw needn't show every extreme that they name: `lengths`: positions from a table's length on are padding; some table has exactly 512 live tokens.
All inputs are finite; a program needn't handle non-finite values.
Results may differ from a plain program's by a relative error of at most 0.018.
Values may be sent and summed in bfloat16 or wider, within the bound.
A program may use at most 256 MiB of HBM per device.

v0:
```python
import math
from functools import partial

import jax
import jax.numpy as jnp
from jax import lax
from jax.experimental import pallas as pl
from jax.experimental.pallas import tpu as pltpu
from jax.sharding import PartitionSpec as P

D = 768
H = 12
HD = 64
LEN = 512
FF = 3072
PAIR = 2 * HD

EPS = 1e-06
NEGATIVE = -1e30
BETA_ONE = 0.9
BETA_TWO = 0.999
ADAM_EPS = 1e-08
DECAY = 0.01
RATES = (1.0, 15.0, 1.0, 0.5, 5.0)

F32 = jnp.float32
BF16 = jnp.bfloat16
MESH_ID = pl.DeviceIdType.MESH
VMEM_ALL = 64 * 1000 * 1024


def layer_norm(hidden, gain_vec, shift_vec):
    row_mean = jnp.mean(hidden, axis=-1, keepdims=True)
    centred = hidden - row_mean
    variance = jnp.mean(centred * centred, axis=-1, keepdims=True)
    return centred * lax.rsqrt(variance + EPS) * gain_vec + shift_vec


def inner(left, right):
    return lax.dot_general(left, right, (((0,), (0,)), ((), ())), preferred_element_type=F32)


def back_mul(left, right):
    return lax.dot_general(left, right, (((1,), (1,)), ((), ())), preferred_element_type=F32)


def adam(master, gradient, first_moment, second_moment, rate_now, step_float):
    moment_new = BETA_ONE * first_moment + (1.0 - BETA_ONE) * gradient
    square_new = BETA_TWO * second_moment + (1.0 - BETA_TWO) * gradient * gradient
    fix_one = 1.0 - jnp.power(BETA_ONE, step_float)
    fix_two = 1.0 - jnp.power(BETA_TWO, step_float)
    update = moment_new / fix_one / (jnp.sqrt(square_new / fix_two) + ADAM_EPS)
    master_new = master - rate_now * (update + DECAY * master)
    return (moment_new, square_new, master_new, master_new.astype(BF16))


def head_masks(dtype):
    lane = lax.broadcasted_iota(jnp.int32, (1, PAIR), 1)
    return [(lane < HD).astype(dtype), (lane >= HD).astype(dtype)]


def attn_fwd_kernel(len_ref, q_ref, k_ref, v_ref, o_ref, l_ref):
    live = len_ref[pl.program_id(0)]
    masks = head_masks(BF16)
    keys = k_ref[...]
    values = v_ref[...]
    rows = 256
    key_at = lax.broadcasted_iota(jnp.int32, (1, LEN), 1)
    bias = jnp.where(key_at < live, 0.0, NEGATIVE)
    lane = lax.broadcasted_iota(jnp.int32, (1, PAIR), 1)
    for start in range(0, LEN, rows):
        query = q_ref[pl.ds(start, rows), :] * jnp.asarray(HD ** (-0.5), BF16)
        mixed, logs = [], []
        for head in range(2):
            scores = back_mul(query * masks[head], keys) + bias
            top = jnp.max(scores, axis=-1, keepdims=True)
            raised = jnp.exp(scores - top)
            total = jnp.sum(raised, axis=-1, keepdims=True)
            probs = (raised * (1.0 / total)).astype(BF16)
            mixed.append(jnp.dot(probs, values, preferred_element_type=F32))
            logs.append(top + jnp.log(total))
        o_ref[pl.ds(start, rows), :] = jnp.where(lane < HD, mixed[0], mixed[1]).astype(BF16)
        both = jnp.where(lane < HD, logs[0], logs[1])
        flat = both.T
        l_ref[0, 0, 0:1, pl.ds(start, rows)] = flat[0:1, :]
        l_ref[0, 0, 1:2, pl.ds(start, rows)] = flat[HD : HD + 1, :]


def attention_forward(lengths, qkv, tables):
    pairs = H // 2
    spec = lambda part: pl.BlockSpec((LEN, PAIR), lambda t, h, n: (t, part * pairs + h))
    return pl.pallas_call(
        attn_fwd_kernel,
        grid_spec=pltpu.PrefetchScalarGridSpec(
            num_scalar_prefetch=1,
            grid=(tables, pairs),
            in_specs=[spec(0), spec(1), spec(2)],
            out_specs=[
                pl.BlockSpec((LEN, PAIR), lambda t, h, n: (t, h)),
                pl.BlockSpec((1, 1, 8, LEN), lambda t, h, n: (t, h, 0, 0)),
            ],
        ),
        out_shape=[
            jax.ShapeDtypeStruct((tables * LEN, D), BF16),
            jax.ShapeDtypeStruct((tables, pairs, 8, LEN), F32),
        ],
        name="attn_fwd",
    )(lengths, qkv, qkv, qkv)


def attn_bwd_kernel(len_ref, q_ref, k_ref, v_ref, o_ref, l_ref, do_ref, d_ref, sums_ref):
    live = len_ref[pl.program_id(0)]
    masks = head_masks(BF16)
    keys = k_ref[...]
    values = v_ref[...]
    query = q_ref[...] * jnp.asarray(HD ** (-0.5), BF16)
    grad_out = do_ref[...]
    dots = (grad_out.astype(F32) * o_ref[...].astype(F32)).T
    rows = 256
    q_masked = [query * m for m in masks]
    g_masked = [grad_out * m for m in masks]
    deltas = [jnp.sum(dots[h * HD : (h + 1) * HD, :], axis=0, keepdims=True) for h in range(2)]
    logs = [l_ref[0, 0, h : h + 1, :] for h in range(2)]
    grad_q = jnp.zeros((LEN, PAIR), F32)
    sum_v = jnp.zeros((1, PAIR), F32)
    for start in range(0, LEN, rows):
        part_k = keys[start : start + rows, :]
        part_v = values[start : start + rows, :]
        key_at = start + lax.broadcasted_iota(jnp.int32, (rows, 1), 0)
        bias = jnp.where(key_at < live, 0.0, NEGATIVE)
        grad_k = jnp.zeros((rows, PAIR), F32)
        grad_v = jnp.zeros((rows, PAIR), F32)
        for head in range(2):
            scores = back_mul(part_k, q_masked[head])
            probs = jnp.exp(scores + bias - logs[head])
            grad_probs = back_mul(part_v, g_masked[head])
            grad_s = (probs * (grad_probs - deltas[head])).astype(BF16)
            grad_v += jnp.dot(probs.astype(BF16), g_masked[head], preferred_element_type=F32)
            grad_k += jnp.dot(grad_s, q_masked[head], preferred_element_type=F32)
            grad_q += inner(grad_s, part_k * masks[head])
        d_ref[1, pl.ds(start, rows), :] = grad_k.astype(BF16)
        d_ref[2, pl.ds(start, rows), :] = grad_v.astype(BF16)
        sum_v += jnp.sum(grad_v, axis=0, keepdims=True)
    grad_q = grad_q * HD ** (-0.5)
    d_ref[0, :, :] = grad_q.astype(BF16)
    sums_ref[0, 0, 0:1, :] = jnp.sum(grad_q, axis=0, keepdims=True)
    sums_ref[0, 0, 1:2, :] = sum_v


def attention_backward(lengths, qkv, mixed, logs, grad_mixed, tables):
    pairs = H // 2
    spec = lambda part: pl.BlockSpec((LEN, PAIR), lambda t, h, n: (t, part * pairs + h))
    block = pl.BlockSpec((LEN, PAIR), lambda t, h, n: (t, h))
    return pl.pallas_call(
        attn_bwd_kernel,
        grid_spec=pltpu.PrefetchScalarGridSpec(
            num_scalar_prefetch=1,
            grid=(tables, pairs),
            in_specs=[
                spec(0),
                spec(1),
                spec(2),
                block,
                pl.BlockSpec((1, 1, 8, LEN), lambda t, h, n: (t, h, 0, 0)),
                block,
            ],
            out_specs=[
                pl.BlockSpec((3, LEN, PAIR), lambda t, h, n: (0, t, h)),
                pl.BlockSpec((1, 1, 8, PAIR), lambda t, h, n: (t, h, 0, 0)),
            ],
        ),
        out_shape=[
            jax.ShapeDtypeStruct((3, tables * LEN, D), BF16),
            jax.ShapeDtypeStruct((tables, pairs, 8, PAIR), F32),
        ],
        name="attn_bwd",
    )(lengths, qkv, qkv, qkv, mixed, logs, grad_mixed)


def place():
    tab, blk = lax.axis_index("tab"), lax.axis_index("blk")
    return tab // 2, tab % 2, blk // 2, blk % 2


def z_line():
    z = place()[0]
    inner = (z + 1) // 2 % 2
    near = inner * (z - 1) * 3 + (1 - inner) * (1 + z // 3)
    second = inner * (3 - z) + (1 - inner) * (3 - near)
    third = inner * (3 - near) + (1 - inner) * (3 - z)
    return inner, near, (near, second, third)


def greet(peers):
    barrier = pltpu.get_barrier_semaphore()
    for z, x, y, c in peers:
        pl.semaphore_signal(
            barrier, inc=1, device_id=(z * 2 + x, y * 2 + c), device_id_type=MESH_ID
        )
    pl.semaphore_wait(barrier, len(peers))


def all_peers():
    z, x, y, c = place()
    z_peers = [((z + j) % 4, x, y, c) for j in range(1, 4)]
    rest = [(z, 1 - x, y, c), (z, x, 1 - y, c), (z, x, y, 1 - c), (z, x, 1 - y, 1 - c)]
    return z_peers + rest


def by_columns(width):
    return lambda ref, t, part: ref.at[t, :, pl.ds(pl.multiple_of(part * width, 128), width)]


def by_rows(height):
    return lambda ref, t, part: ref.at[t, pl.ds(pl.multiple_of(part * height, 16), height), :]


PIECES = (
    (by_columns(3 * D // 2), False),
    (by_columns(D // 2), False),
    (by_columns(FF // 4), True),
    (by_rows(FF // 16), False),
)
G_WIRES = 96
STEPS = 12


class Gather:
    def __init__(self, at, shard, whole, plan):
        piece, self.split = PIECES[at]
        z, x, y, c = place()
        tab = z * 2 + x
        part = y * 2 + c if self.split else c
        other = (1 - y) * 2 + c
        own = lambda: piece(shard, 0, part)
        self.plan = plan
        self.middle, outer, order = z_line()
        near = lambda j: order[j - 1] * 2 + x
        far = lambda j: order[j - 1] * 2 + 1 - x if j else z * 2 + 1 - x

        def send(at_tab, which, to, first=False, inner=False):
            return plan.add(
                lambda: (
                    own() if first else piece(whole, at_tab, which),
                    piece(whole, at_tab, which),
                    to,
                ),
                inner,
            )

        side, over, across = (z, x, y, 1 - c), (z, x, 1 - y, c), (z, 1 - x, y, c)
        to_outer, to_inner = (outer, x, y, c), (3 - z, x, y, c)
        self.own_near = send(tab, part, to_outer, True)
        self.own_inner = send(tab, part, to_inner, True, inner=True)
        self.passed = [
            send(near(j), part, to_inner if j == 1 else to_outer, inner=True) for j in range(1, 4)
        ]
        self.x = [send(tab, part, across, True)]
        self.x += [send(near(j), part, across) for j in range(1, 4)]
        tabs = [near(j) for j in range(1, 4)] + [far(j) for j in range(4)]
        self.c = [send(t, part, side) for t in tabs]
        self.y = [send(t, part, over) for t in tabs] if self.split else []
        self.late = [send(t, other, side) for t in tabs] if self.split else []

    def send_z(self):
        self.plan.start(self.own_near)

        @pl.when(self.middle == 1)
        def _():
            self.plan.start(self.own_inner)

    def send_x(self):
        self.plan.start(self.x[0])

    def onward(self, at):
        if self.split:
            self.plan.start(self.y[at])
        self.plan.start(self.c[at])

    def task_z(self, j):
        if j == 1:
            self.plan.arrived(self.own_near)
        else:

            @pl.when(self.middle == 0)
            def _():
                self.plan.arrived(self.passed[j - 1])

        @pl.when(self.middle == 1)
        def _():
            if j > 1:
                self.plan.arrived(self.own_inner if j == 2 else self.passed[0])
            self.plan.start(self.passed[j - 1])

        self.plan.start(self.x[j])
        self.onward(j - 1)

    def task_x(self, j):
        self.plan.arrived(self.x[j])
        self.onward(3 + j)

    def task_y(self, at):
        self.plan.arrived(self.y[at])
        self.plan.start(self.late[at])

    def end(self):
        for index in self.c + self.late:
            self.plan.arrived(index)


def gather_kernel(
    len_ref, x_in, cot_in, qkv_wide, out_wide, up_wide, down_wide, vec_in,
    x_out, cot_out, qkv_out, out_out, up_out, down_out, vec_out, acts_out, mixed_out, logs_out,
    qkv_in, out_in, up_in, down_in, x_all, w_all, vec_all, acts, mixed, logs, bias,
    send, recv, own,
):
    z, x, y, c = place()
    tab, blk = z * 2 + x, y * 2 + c
    share, span = x_in.shape[0] // 4, x_in.shape[1]
    mine = pl.ds(blk * share, share)
    slot = pl.ds(pl.multiple_of(blk * span, span), span)
    plan = Plan(send, recv)
    shards = (qkv_in, out_in, up_in, down_in)
    wholes = (w_all, out_out, up_out, down_out)
    works = [Gather(at, shards[at], wholes[at], plan) for at in range(4)]
    qkv, out, up, down = works

    def trade(src, dst):
        made = []
        for other in ((z, x, 1 - y, c), (z, x, 1 - y, 1 - c), (z, x, y, 1 - c)):
            their = other[2] * 2 + other[3]
            made.append(
                plan.add(
                    lambda their=their, other=other: (
                        src.at[pl.ds(their * share, share)], dst.at[:, slot, :], other,
                    )
                )
            )
        return made

    trade_x, trade_cot = trade(x_in, x_all), trade(cot_in, cot_out)
    vec_z = [
        plan.add(lambda j=j: (vec_in.at[0], vec_all.at[tab], ((z + j) % 4, x, y, c)))
        for j in range(1, 4)
    ]
    vec_x = [plan.add(lambda: (vec_in.at[0], vec_all.at[tab], (z, 1 - x, y, c)))]
    for j in range(1, 4):
        t = (z + 4 - j) % 4 * 2 + x
        vec_x.append(plan.add(lambda t=t: (vec_all.at[t], vec_all.at[t], (z, 1 - x, y, c))))
    keeps = [
        lambda: pltpu.make_async_copy(x_in.at[mine], x_all.at[:, slot, :], own.at[0]),
        lambda: pltpu.make_async_copy(qkv_in.at[0], w_all.at[tab], own.at[1]),
        lambda: pltpu.make_async_copy(vec_in.at[0], vec_all.at[tab], own.at[2]),
        lambda: pltpu.make_async_copy(cot_in.at[mine], cot_out.at[:, slot, :], own.at[3]),
        lambda: pltpu.make_async_copy(out_in.at[0], out_out.at[tab], own.at[4]),
        lambda: pltpu.make_async_copy(up_in.at[0], up_out.at[tab], own.at[5]),
        lambda: pltpu.make_async_copy(down_in.at[0], down_out.at[tab], own.at[6]),
    ]
    puts = [
        lambda: pltpu.make_async_copy(x_all, x_out, own.at[7]),
        lambda: pltpu.make_async_copy(w_all, qkv_out, own.at[8]),
        lambda: pltpu.make_async_copy(vec_all, vec_out, own.at[9]),
        lambda: pltpu.make_async_copy(acts, acts_out, own.at[10]),
        lambda: pltpu.make_async_copy(mixed, mixed_out, own.at[11]),
        lambda: pltpu.make_async_copy(logs, logs_out, own.at[12]),
    ]
    for wide, narrow in zip((qkv_wide, out_wide, up_wide, down_wide), shards):

        def rounded(i, carry, wide=wide, narrow=narrow):
            rows = pl.ds(pl.multiple_of(i * 16, 16), 16)
            narrow[0, rows, :] = wide[rows, :].astype(BF16)
            return carry

        lax.fori_loop(0, wide.shape[0] // 16, rounded, 0)
    greet(all_peers())
    for index in vec_z + vec_x[:1]:
        plan.start(index)
    qkv.send_z()
    qkv.send_x()
    for index in trade_x:
        plan.start(index)
    for keep in keeps:
        keep().start()
    for work in (out, up, down):
        work.send_z()
    out.send_x()
    for index in trade_cot:
        plan.start(index)
    for j in range(1, 4):
        plan.arrived(vec_z[j - 1])
        plan.start(vec_x[j])
    for j in range(1, 4):
        qkv.task_z(j)
    up.send_x()
    down.send_x()
    for j in range(4):
        qkv.task_x(j)
    for index in vec_x:
        plan.arrived(index)
    for keep in keeps[:3]:
        keep().wait()
    for index in trade_x:
        plan.arrived(index)
    qkv.end()
    for put in puts[:3]:
        put().start()

    tile = 256
    rows = share * LEN
    spread = [vec_all[t, 0:16, :].astype(F32) for t in range(8)]
    vectors = spread[0]
    for t in range(1, 8):
        vectors = vectors + spread[t]
    bias[:, 0:D] = vectors[0:1, :]
    bias[:, D : 2 * D] = jnp.zeros((1, D), F32)
    bias[:, 2 * D : 3 * D] = vectors[1:2, :]

    def project(i, carry):
        cols = pl.ds(pl.multiple_of(i * tile, tile), tile)
        weight = w_all[:, :, cols].reshape(D, tile)
        value = jnp.dot(x_all[...].reshape(rows, D), weight, preferred_element_type=F32)
        acts[:, cols] = (value + bias[:, cols]).astype(BF16)
        return carry

    lax.fori_loop(0, 3 * D // tile, project, 0)
    puts[3]().start()

    tasks = {
        0: [lambda j=j: out.task_z(j) for j in (1, 2, 3)],
        1: [lambda: up.task_z(1), lambda: up.task_z(2)],
        2: [lambda j=j: out.task_x(j) for j in range(4)] + [lambda: up.task_z(3)],
        3: [lambda: up.task_x(0)],
        4: [lambda: down.task_z(1)],
        5: [lambda: down.task_z(2), lambda: up.task_x(1)],
        6: [lambda: down.task_x(0), lambda: up.task_x(2)],
        7: [lambda: down.task_z(3)],
        8: [lambda: up.task_x(3), lambda: up.task_y(0)],
        9: [lambda: up.task_y(1), lambda: down.task_x(1)],
        10: [lambda: up.task_y(2), lambda: up.task_y(3)],
        11: [lambda: up.task_y(4), lambda: down.task_x(2)],
        12: [lambda: up.task_y(5), lambda: up.task_y(6), lambda: down.task_x(3)],
    }

    def step(s, carry):
        for when, todo in tasks.items():
            if when < STEPS:

                @pl.when(s == when)
                def _(todo=todo):
                    for task in todo:
                        task()

        t, h = s // (STEPS // share), s % (STEPS // share)
        base = pl.multiple_of(t * LEN, LEN)
        cols = [pl.ds(pl.multiple_of(part * D + h * PAIR, PAIR), PAIR) for part in range(3)]
        attend(len_ref[t], acts, mixed, logs, t, h, base, cols)
        return carry

    lax.fori_loop(0, STEPS, step, 0)
    for put in puts[4:]:
        put().start()
    for task in tasks[STEPS]:
        task()
    for index in trade_cot:
        plan.arrived(index)
    for work in (out, up, down):
        work.end()
    plan.finish(z_line()[0])
    for keep in keeps[3:]:
        keep().wait()
    for put in puts:
        put().wait()


def attend(live, acts, mixed_ref, logs_ref, t, h, base, cols):
    masks = head_masks(BF16)
    keys = acts[pl.ds(base, LEN), cols[1]]
    values = acts[pl.ds(base, LEN), cols[2]]
    rows = 256
    key_at = lax.broadcasted_iota(jnp.int32, (1, LEN), 1)
    bias = jnp.where(key_at < live, 0.0, NEGATIVE)
    lane = lax.broadcasted_iota(jnp.int32, (1, PAIR), 1)

    def half(i, carry):
        at = pl.ds(pl.multiple_of(base + i * rows, rows), rows)
        query = acts[at, cols[0]] * jnp.asarray(HD ** (-0.5), BF16)
        mixed, logs = [], []
        for head in range(2):
            scores = back_mul(query * masks[head], keys) + bias
            top = jnp.max(scores, axis=-1, keepdims=True)
            raised = jnp.exp(scores - top)
            total = jnp.sum(raised, axis=-1, keepdims=True)
            probs = (raised * (1.0 / total)).astype(BF16)
            mixed.append(jnp.dot(probs, values, preferred_element_type=F32))
            logs.append(top + jnp.log(total))
        mixed_ref[at, cols[0]] = jnp.where(lane < HD, mixed[0], mixed[1]).astype(BF16)
        flat = jnp.where(lane < HD, logs[0], logs[1]).T
        to = pl.ds(pl.multiple_of(i * rows, rows), rows)
        logs_ref[t, h, 0:1, to] = flat[0:1, :]
        logs_ref[t, h, 1:2, to] = flat[HD : HD + 1, :]
        return carry

    lax.fori_loop(0, LEN // rows, half, 0)


def gather_all(lengths, tables, cotangent, qkv, out, up, down, vec):
    share, span = tables.shape[0] // 4, tables.shape[1] * 4
    vmem = pl.BlockSpec(memory_space=pltpu.VMEM)
    hbm = pl.BlockSpec(memory_space=pl.ANY)
    shape = lambda a: jax.ShapeDtypeStruct((8,) + a.shape[-2:], BF16)
    rows = share * span
    logs = (share, STEPS // share, 8, LEN)
    return pl.pallas_call(
        gather_kernel,
        in_specs=[pl.BlockSpec(memory_space=pltpu.SMEM)] + [vmem] * 7,
        out_specs=[hbm] * 10,
        out_shape=[
            jax.ShapeDtypeStruct((share, span, D), BF16),
            jax.ShapeDtypeStruct((share, span, D), BF16),
            shape(qkv), shape(out), shape(up), shape(down), shape(vec),
            jax.ShapeDtypeStruct((rows, 3 * D), BF16),
            jax.ShapeDtypeStruct((rows, D), BF16),
            jax.ShapeDtypeStruct(logs, F32),
        ],
        scratch_shapes=[
            *[pltpu.VMEM((1,) + w.shape, BF16) for w in (qkv, out, up, down)],
            pltpu.VMEM((share, span, D), BF16),
            pltpu.VMEM((8,) + qkv.shape, BF16),
            pltpu.VMEM((8,) + vec.shape[1:], BF16),
            pltpu.VMEM((rows, 3 * D), BF16),
            pltpu.VMEM((rows, D), BF16),
            pltpu.VMEM(logs, F32),
            pltpu.VMEM((1, 3 * D), F32),
            pltpu.SemaphoreType.DMA((G_WIRES,)),
            pltpu.SemaphoreType.DMA((G_WIRES,)),
            pltpu.SemaphoreType.DMA((13,)),
        ],
        compiler_params=pltpu.CompilerParams(
            collective_id=0, has_side_effects=True, vmem_limit_bytes=VMEM_ALL
        ),
        name="gather_attend",
    )(lengths, tables, cotangent, qkv, out, up, down, vec)


class Plan:
    def __init__(self, send, recv):
        self.send, self.recv, self.makers, self.inner = send, recv, [], []

    def add(self, maker, inner=False):
        self.makers.append(maker)
        if inner:
            self.inner.append(len(self.makers) - 1)
        return len(self.makers) - 1

    def build(self, index):
        src, dst, (z, x, y, c) = self.makers[index]()
        return pltpu.make_async_remote_copy(
            src_ref=src,
            dst_ref=dst,
            send_sem=self.send.at[index],
            recv_sem=self.recv.at[index],
            device_id=(z * 2 + x, y * 2 + c),
            device_id_type=MESH_ID,
        )

    def start(self, index):
        self.build(index).start()

    def arrived(self, index):
        self.build(index).wait_recv()

    def finish(self, inner):
        for index in range(len(self.makers)):
            if index not in self.inner:
                self.build(index).wait_send()

        @pl.when(inner == 1)
        def _():
            for index in self.inner:
                self.build(index).wait_send()


class Slab:
    def __init__(self, rows, cols, split, axis, first=0, dtype=BF16):
        self.rows, self.cols, self.split, self.axis = rows, cols, split, axis
        self.first, self.dtype = first, dtype
        self.tile = 128 if axis == 1 else (16 if dtype == BF16 else 8)

    def cut(self, index):
        size = self.cols if self.axis == 1 else self.rows
        part = pl.ds(pl.multiple_of(self.first + index * size, self.tile), size)
        if self.axis == 1:
            return pl.ds(0, self.rows), part
        return part, pl.ds(0, self.cols)

    def scratch(self):
        ways = 2 if self.split else 1
        vmem = lambda *lead: pltpu.VMEM(lead + (self.rows, self.cols), self.dtype)
        late = vmem(4, 2) if self.split else vmem(1, 1)
        return [vmem(ways, 4, 2), vmem(ways, 4, 2), late, vmem(4), vmem(5), vmem()]

    def copies(self):
        return (2 if self.split else 1) + 1 + 1 + 4 + 3


class Reduction:
    def __init__(self, slab, source, target, scratch, plan, own, own_at):
        self.slab, self.source, self.target, self.plan = slab, source, target, plan
        self.held, self.from_c, self.from_y, self.from_x, self.from_z, self.done = scratch
        self.own, self.own_at = own, own_at
        z, x, y, c = place()
        self.at = z, x, y, c
        self.slot = y if slab.split else 0
        side = (z, x, y, 1 - c)
        over = (z, x, 1 - y, c)

        def index_of(half, core):
            return half * 2 + core if slab.split else core

        def cut_all(ref, index):
            rows, cols = slab.cut(index)
            return ref.at[:, :, rows, cols]

        def cut_out(index):
            rows, cols = slab.cut(index)
            return target.at[rows, cols]

        ways = 2 if slab.split else 1
        self.loads = [
            lambda half=half: pltpu.make_async_copy(
                cut_all(source, index_of(half, c)), self.held.at[half], own.at[own_at + half]
            )
            for half in range(ways)
        ]
        self.to_core = [
            plan.add(
                lambda half=half: (
                    cut_all(source, index_of(half, 1 - c)), self.from_c.at[half], side,
                )
            )
            for half in range(ways)
        ]
        if slab.split:
            self.to_y = plan.add(lambda: (self.held.at[1 - y], self.from_y, over))
        else:
            self.to_y = plan.add(lambda: (self.done, self.from_y.at[0, 0], over))
        self.to_x = plan.add(
            lambda: (self.held.at[self.slot, :, 1 - x], self.from_x, (z, 1 - x, y, c))
        )
        self.middle, outer, _ = z_line()
        self.outer = outer
        self.inward = 2 - z // 2 * 2
        to_outer, to_inner = (outer, x, y, c), (3 - z, x, y, c)
        owned_by = lambda at: self.held.at[self.slot, at, x]
        beyond = lambda: self.held.at[self.slot, pl.ds(self.inward, 2), x]
        self.out_in = plan.add(lambda: (beyond(), self.from_z.at[pl.ds(0, 2)], to_outer))
        self.out_near = plan.add(lambda: (owned_by(outer), self.from_z.at[2], to_outer))
        self.in_in = plan.add(lambda: (beyond(), self.from_z.at[pl.ds(3, 2)], to_inner))
        self.in_out = plan.add(lambda: (owned_by(outer), self.from_z.at[0], to_outer))
        mine = lambda: cut_out(index_of(y, c))
        self.store = lambda: pltpu.make_async_copy(self.done, mine(), own.at[own_at + 2])
        self.share_core = plan.add(lambda: (self.done, mine(), side))
        if slab.split:
            theirs = lambda: cut_out(index_of(1 - y, c))
            self.share_y = plan.add(lambda: (self.done, mine(), over))
            self.share_far = plan.add(lambda: (theirs(), theirs(), side))

    def begin(self):
        for load in self.loads:
            load().start()
        for index in self.to_core:
            self.plan.start(index)

    def summed(self, total, *others, into=None):
        into = total if into is None else into

        def step(i, carry):
            rows = pl.ds(pl.multiple_of(i * 16, 16), 16)
            value = total[rows, :].astype(F32)
            for other in others:
                value = value + other[rows, :].astype(F32)
            into[rows, :] = value.astype(self.slab.dtype)
            return carry

        lax.fori_loop(0, self.slab.rows // 16, step, 0)

    def after_core(self):
        for half, load in enumerate(self.loads):
            load().wait()
            self.plan.arrived(self.to_core[half])

        def step(t, carry):
            for half in range(len(self.loads)):
                self.summed(self.held.at[half, t // 2, t % 2], self.from_c.at[half, t // 2, t % 2])
            return carry

        lax.fori_loop(0, 8, step, 0)
        self.plan.start(self.to_y if self.slab.split else self.to_x)

    def after_y(self):
        if not self.slab.split:
            return
        self.plan.arrived(self.to_y)

        def step(t, carry):
            self.summed(self.held.at[self.slot, t // 2, t % 2], self.from_y.at[t // 2, t % 2])
            return carry

        lax.fori_loop(0, 8, step, 0)
        self.plan.start(self.to_x)

    def after_x(self):
        z, x, y, c = self.at
        self.plan.arrived(self.to_x)

        def step(t, carry):
            self.summed(self.held.at[self.slot, t, x], self.from_x.at[t])
            return carry

        lax.fori_loop(0, 4, step, 0)

        @pl.when(self.middle == 0)
        def _():
            self.plan.start(self.out_in)
            self.plan.start(self.out_near)

    def after_a(self):
        @pl.when(self.middle == 1)
        def _():
            self.plan.arrived(self.out_in)
            for at in range(2):
                total = self.held.at[self.slot, self.inward + at, self.at[1]]
                self.summed(total, self.from_z.at[at])
            self.plan.start(self.in_in)

    def after_b(self):
        @pl.when(self.middle == 1)
        def _():
            self.plan.arrived(self.in_in)
            at = 3 + self.outer - (2 - self.inward)
            total = self.held.at[self.slot, self.outer, self.at[1]]
            self.summed(total, self.from_z.at[at])
            self.plan.start(self.in_out)

    def after_z(self):
        z, x, y, c = self.at

        @pl.when(self.middle == 1)
        def _():
            self.plan.arrived(self.out_near)
            other = self.from_z.at[3 + z - (2 - self.inward)]
            own = self.held.at[self.slot, z, x]
            self.summed(own, self.from_z.at[2], other, into=self.done)

        @pl.when(self.middle == 0)
        def _():
            self.plan.arrived(self.in_out)
            self.summed(self.held.at[self.slot, z, x], self.from_z.at[0], into=self.done)

        if self.slab.split:
            self.plan.start(self.share_y)
            self.plan.start(self.share_core)
            self.store().start()
        else:
            self.plan.start(self.to_y)

    def after_final(self):
        if self.slab.split:
            self.plan.arrived(self.share_y)
            self.plan.start(self.share_far)
        else:
            self.plan.arrived(self.to_y)
            self.plan.build(self.to_y).wait_send()
            self.summed(self.done, self.from_y.at[0, 0])
            self.plan.start(self.share_core)
            self.store().start()

    def end(self):
        self.plan.arrived(self.share_core)
        if self.slab.split:
            self.plan.arrived(self.share_far)
        self.store().wait()

    def finish_sends(self):
        done_early = () if self.slab.split else (self.to_y,)
        sends = self.to_core + [self.to_y, self.to_x, self.share_core]
        if self.slab.split:
            sends += [self.share_y, self.share_far]
        for index in sends:
            if index not in done_early:
                self.plan.build(index).wait_send()

        @pl.when(self.middle == 1)
        def _():
            self.plan.build(self.in_in).wait_send()
            self.plan.build(self.in_out).wait_send()

        @pl.when(self.middle == 0)
        def _():
            self.plan.build(self.out_in).wait_send()
            self.plan.build(self.out_near).wait_send()


SLABS = {
    "down_y": (1, Slab(64, D, True, 0)),
    "up_low": (0, Slab(96, D // 2, True, 1)),
    "down": (1, Slab(64, D, False, 0, first=256)),
    "up_high": (0, Slab(96, D, False, 1, first=2 * D)),
    "out": (3, Slab(96, D // 2, False, 1)),
    "v": (2, Slab(96, D // 2, False, 1, first=2 * D)),
    "k": (2, Slab(96, D // 2, False, 1, first=D)),
    "q": (2, Slab(96, D // 2, False, 1)),
}


def attend_back(live, acts, mixed_ref, logs_ref, do_ref, d_ref, vec_ref, t, h, base, cols):
    masks = head_masks(BF16)
    rows_all = pl.ds(base, LEN)
    keys = acts[rows_all, cols[1]]
    values = acts[rows_all, cols[2]]
    query = acts[rows_all, cols[0]] * jnp.asarray(HD ** (-0.5), BF16)
    grad_out = do_ref[rows_all, cols[0]]
    dots = (grad_out.astype(F32) * mixed_ref[rows_all, cols[0]].astype(F32)).T
    rows = 256
    q_masked = [query * m for m in masks]
    g_masked = [grad_out * m for m in masks]
    deltas = [jnp.sum(dots[i * HD : (i + 1) * HD, :], axis=0, keepdims=True) for i in range(2)]
    logs = [logs_ref[t, h, i : i + 1, :] for i in range(2)]
    grad_q = jnp.zeros((LEN, PAIR), F32)
    sum_v = jnp.zeros((1, PAIR), F32)
    for start in range(0, LEN, rows):
        part_k = keys[start : start + rows, :]
        part_v = values[start : start + rows, :]
        key_at = start + lax.broadcasted_iota(jnp.int32, (rows, 1), 0)
        bias = jnp.where(key_at < live, 0.0, NEGATIVE)
        grad_k = jnp.zeros((rows, PAIR), F32)
        grad_v = jnp.zeros((rows, PAIR), F32)
        for head in range(2):
            scores = back_mul(part_k, q_masked[head])
            probs = jnp.exp(scores + bias - logs[head])
            grad_probs = back_mul(part_v, g_masked[head])
            grad_s = (probs * (grad_probs - deltas[head])).astype(BF16)
            grad_v += jnp.dot(probs.astype(BF16), g_masked[head], preferred_element_type=F32)
            grad_k += jnp.dot(grad_s, q_masked[head], preferred_element_type=F32)
            grad_q += inner(grad_s, part_k * masks[head])
        d_ref[pl.ds(base + start, rows), cols[1]] = grad_k.astype(BF16)
        d_ref[pl.ds(base + start, rows), cols[2]] = grad_v.astype(BF16)
        sum_v += jnp.sum(grad_v, axis=0, keepdims=True)
    grad_q = grad_q * HD ** (-0.5)
    d_ref[rows_all, cols[0]] = grad_q.astype(BF16)
    vec_ref[0:1, cols[0]] += jnp.sum(grad_q, axis=0, keepdims=True)
    vec_ref[1:2, cols[0]] += sum_v


N_LOADS = 7


def reduce_kernel(
    len_ref, acts_in, mixed_in, do_in, logs_in, x_in, w_in, one_in, y_in, vec_in,
    up_in, down_in, out_in,
    gin_out, y_out, up_out, down_out, qkv_out, out_out, vec_out,
    acts, mixed, do, logs, x_all, w_all, one, x_turned, d, gw, gin, vec, vec_from, *rest,
):
    scratch, (send, recv, own) = rest[:-3], rest[-3:]
    z, x, y, c = place()
    blk = y * 2 + c
    loads = [
        lambda at=at, src=src, dst=dst: pltpu.make_async_copy(src, dst, own.at[at])
        for at, (src, dst) in enumerate(
            (
                (acts_in, acts), (mixed_in, mixed), (do_in, do), (logs_in, logs),
                (x_in, x_all), (w_in, w_all), (one_in, one),
            )
        )
    ]
    for load in loads:
        load().start()
    greet(all_peers())
    plan = Plan(send, recv)
    share, span = gin_out.shape[0] // 4, gin_out.shape[1]
    sources, targets = (up_in, down_in, gw, out_in), (up_out, down_out, qkv_out, out_out)
    works = {}
    for at, (name, (number, slab)) in enumerate(SLABS.items()):
        part = scratch[6 * at : 6 * at + 6]
        works[name] = Reduction(
            slab, sources[number], targets[number], part, plan, own, N_LOADS + 2 + 3 * at
        )
    mine = pl.ds(blk * share, share)
    slot = pl.ds(pl.multiple_of(blk * span, span), span)
    kept = [
        lambda at=at, src=src, dst=dst: pltpu.make_async_copy(
            src.at[:, slot, :], dst.at[mine], own.at[N_LOADS + at]
        )
        for at, (src, dst) in enumerate(((gin, gin_out), (y_in, y_out)))
    ]

    def trade(src, dst):
        made = []
        for other in ((z, x, 1 - y, c), (z, x, 1 - y, 1 - c), (z, x, y, 1 - c)):
            their = other[2] * 2 + other[3]
            made.append(
                plan.add(
                    lambda their=their, other=other: (
                        src.at[:, pl.ds(pl.multiple_of(their * span, span), span), :],
                        dst.at[mine],
                        other,
                    )
                )
            )
        return made

    trade_g, trade_y = trade(gin, gin_out), trade(y_in, y_out)
    ways = [(z, x, y, 1 - c), (z, x, 1 - y, c), (z, 1 - x, y, c)]
    ways += [((z + j) % 4, x, y, c) for j in range(1, 4)]
    vec_sends = [
        plan.add(lambda at=at, to=to: (vec.at[min(at, 3)], vec_from.at[at], to))
        for at, to in enumerate(ways)
    ]

    def vec_task(at):
        if at == 0:
            plan.start(vec_sends[0])
            return
        plan.arrived(vec_sends[at - 1])
        vec[at] = vec[at - 1] + vec_from[at - 1]
        for index in vec_sends[at:] if at == 3 else vec_sends[at : at + 1]:
            plan.start(index)

    def vec_end():
        for index in vec_sends[3:]:
            plan.arrived(index)
        vec_out[...] = vec[3] + vec_from[3] + vec_from[4] + vec_from[5]

    def do_tasks(todo):
        for entry in todo:
            if entry[0] == "vec":
                vec_task(entry[1])
            elif entry[0] == "trade":
                for index in trade_y:
                    plan.start(index)
            else:
                getattr(works[entry[0]], entry[1])()

    vec[0] = vec_in[...]
    for name in ("down_y", "down", "up_low", "up_high", "out"):
        works[name].begin()
    kept[1]().start()
    for load in loads[:4]:
        load().wait()

    def step(s, carry):
        for when, todo in DURING.items():

            @pl.when(s == when)
            def _(todo=todo):
                do_tasks(todo)

        t, h = s // (STEPS // share), s % (STEPS // share)
        base = pl.multiple_of(t * LEN, LEN)
        cols = [pl.ds(pl.multiple_of(part * D + h * PAIR, PAIR), PAIR) for part in range(3)]
        attend_back(len_ref[t], acts, mixed, logs, do, d, vec.at[0], t, h, base, cols)
        return carry

    lax.fori_loop(0, STEPS, step, 0)
    do_tasks(AFTER["attention"])
    loads[4]().wait()
    rows = share * LEN
    x_turned[...] = x_all[...].T
    tile = 256
    tiles = D // tile

    def grad_tile(i, carry):
        at = (2 - i // tiles) * tiles + i % tiles
        cols = pl.ds(pl.multiple_of(at * tile, tile), tile)
        value = jnp.dot(x_turned[...], d[:, cols], preferred_element_type=F32)
        gw[:, :, :, cols] = value.astype(BF16).reshape(4, 2, D // 8, tile)
        for part, name in enumerate(("v", "k", "q")):

            @pl.when(i == part * tiles + tiles - 1)
            def _(name=name):
                works[name].begin()
                do_tasks(AFTER[name])

        return carry

    lax.fori_loop(0, 3 * tiles, grad_tile, 0)
    loads[5]().wait()
    loads[6]().wait()

    def token_tile(i, carry):
        cols = pl.ds(pl.multiple_of(i * tile, tile), tile)
        value = back_mul(d[...], w_all[cols, :]) + one[:, cols]
        gin[:, :, cols] = value.astype(BF16).reshape(share, LEN, tile)
        for when in range(D // tile):

            @pl.when(i == when)
            def _(when=when):
                do_tasks(AFTER[when])

        return carry

    lax.fori_loop(0, D // tile, token_tile, 0)
    for index in trade_g:
        plan.start(index)
    kept[0]().start()
    do_tasks(AFTER["end"])
    vec_end()
    for work in works.values():
        work.end()
    for index in trade_g + trade_y:
        plan.arrived(index)
    for work in works.values():
        work.finish_sends()
    for index in trade_g + trade_y + vec_sends:
        plan.build(index).wait_send()
    for made in kept:
        made().wait()


DURING = {
    0: [("down_y", "after_core")],
    1: [("down", "after_core"), ("up_low", "after_core")],
    2: [("up_high", "after_core")],
    3: [("out", "after_core"), ("trade",)],
    7: [("down", "after_x")],
    9: [("down_y", "after_y")],
    11: [("up_high", "after_x")],
}
AFTER = {
    "attention": [("vec", 0), ("down", "after_a")],
    "v": [("vec", 1), ("up_low", "after_y")],
    "k": [("v", "after_core"), ("vec", 2)],
    "q": [("k", "after_core"), ("vec", 3), ("out", "after_x"), ("down", "after_b")],
    0: [("q", "after_core"), ("up_high", "after_a")],
    1: [("down", "after_z"), ("down_y", "after_x")],
    2: [("up_high", "after_b")],
    "end": [
        ("out", "after_a"),
        ("up_low", "after_x"),
        ("down_y", "after_a"),
        ("out", "after_b"),
        ("up_high", "after_z"),
        ("down_y", "after_b"),
        ("up_low", "after_a"),
        ("v", "after_x"),
        ("out", "after_z"),
        ("down_y", "after_z"),
        ("up_low", "after_b"),
        ("v", "after_a"),
        ("k", "after_x"),
        ("up_low", "after_z"),
        ("v", "after_b"),
        ("k", "after_a"),
        ("q", "after_x"),
        ("v", "after_z"),
        ("k", "after_b"),
        ("q", "after_a"),
        ("k", "after_z"),
        ("q", "after_b"),
        ("down", "after_final"),
        ("up_high", "after_final"),
        ("out", "after_final"),
        ("down_y", "after_final"),
        ("up_low", "after_final"),
        ("q", "after_z"),
        ("v", "after_final"),
        ("k", "after_final"),
        ("q", "after_final"),
    ],
}


def reduce_all(lengths, acts, mixed, do, logs, rows, whole, one, result, vec, up, down, out):
    share, length = result.shape[:2]
    vmem = pl.BlockSpec(memory_space=pltpu.VMEM)
    hbm = pl.BlockSpec(memory_space=pl.ANY)
    shape = lambda a: jax.ShapeDtypeStruct(a.shape[2:], a.dtype)
    back = jax.ShapeDtypeStruct((share * 4, length // 4, D), BF16)
    scratch = [s for _, slab in SLABS.values() for s in slab.scratch()]
    wires = 12 + sum(slab.copies() for _, slab in SLABS.values())
    like = lambda a: pltpu.VMEM(a.shape, a.dtype)
    return pl.pallas_call(
        reduce_kernel,
        in_specs=[pl.BlockSpec(memory_space=pltpu.SMEM)] + [hbm] * 7 + [vmem] * 2 + [hbm] * 3,
        out_specs=[hbm] * 6 + [vmem],
        out_shape=[
            back, back, shape(up), shape(down),
            jax.ShapeDtypeStruct((D // 8, 3 * D), BF16),
            shape(out),
            jax.ShapeDtypeStruct((16, D), F32),
        ],
        scratch_shapes=[like(a) for a in (acts, mixed, do, logs, rows, whole, one)]
        + [
            pltpu.VMEM(rows.shape[::-1], BF16),
            pltpu.VMEM(acts.shape, BF16),
            pltpu.VMEM((4, 2, D // 8, 3 * D), BF16),
            pltpu.VMEM((share, length, D), BF16),
            pltpu.VMEM((4, 16, D), F32),
            pltpu.VMEM((6, 16, D), F32),
        ]
        + scratch
        + [
            pltpu.SemaphoreType.DMA((wires,)),
            pltpu.SemaphoreType.DMA((wires,)),
            pltpu.SemaphoreType.DMA((N_LOADS + 2 + 3 * len(SLABS),)),
        ],
        compiler_params=pltpu.CompilerParams(
            collective_id=1, has_side_effects=True, vmem_limit_bytes=VMEM_ALL
        ),
        name="attend_reduce",
    )(lengths, acts, mixed, do, logs, rows, whole, one, result, vec, up, down, out)


def local(*args):
    tables, lengths, cotangent, step_count = args[:4]
    masters, firsts, seconds = args[4:9], args[9:14], args[14:19]
    w_qkv, w_out, w_up, w_down, vectors = masters
    blocks = lax.axis_size("blk")
    shards = lax.axis_size("tab")
    table_count, local_len = tables.shape[:2]
    share = table_count // blocks
    tuned = shards == 8 and blocks == 4
    owned = vectors.shape[0]
    vec_own = jnp.pad(vectors.astype(BF16).T, ((0, 4), (0, 0)))
    my_lengths = lax.dynamic_slice(lengths, (lax.axis_index("blk") * share,), (share,))
    if tuned:
        at_own = (0, lax.axis_index("tab") * owned)
        vec_wide = lax.dynamic_update_slice(jnp.zeros((16, D), BF16), vec_own, at_own)
        mine, cot, *wholes, qkv, mixed, logs = gather_all(
            my_lengths, tables, cotangent, w_qkv, w_out, w_up, w_down, vec_wide[None]
        )
        vec_f = jnp.sum(wholes[4].astype(F32), axis=0)[:12]
    else:
        spread = partial(lax.all_to_all, axis_name="blk", split_axis=0, concat_axis=1, tiled=True)
        mine, cot = spread(tables), spread(cotangent)
        narrow = [w.astype(BF16) for w in (w_qkv, w_out, w_up, w_down)]
        wholes = [lax.all_gather(w, "tab", axis=0) for w in narrow + [vec_own]]
        vec_f = wholes[4][:, :12].transpose(1, 0, 2).reshape(12, D).astype(F32)
    full_qkv, full_out, full_up, full_down = [
        w.reshape(-1, w.shape[-1]) for w in wholes[:4]
    ]
    bias_up = vec_f[8:12].reshape(-1)
    rows = mine.reshape(-1, D)
    if not tuned:
        bias_qkv = jnp.concatenate([vec_f[0], jnp.zeros((D,), F32), vec_f[1]])
        qkv = (jnp.dot(rows, full_qkv, preferred_element_type=F32) + bias_qkv).astype(BF16)
        mixed, logs = attention_forward(my_lengths, qkv, share)
    attn_out = jnp.dot(mixed, full_out, preferred_element_type=F32) + vec_f[2]
    normed_one, norm_one_back = jax.vjp(
        layer_norm, rows.astype(F32) + attn_out, vec_f[4], vec_f[5]
    )
    normed_b = normed_one.astype(BF16)
    hidden = jnp.dot(normed_b, full_up, preferred_element_type=F32) + bias_up
    below = 0.5 * (1.0 + lax.erf(hidden * 0.5**0.5))
    active_b = (hidden * below).astype(BF16)
    slope = below + hidden * jnp.exp(-0.5 * hidden * hidden) * (2.0 * math.pi) ** -0.5
    active_b, slope = lax.optimization_barrier((active_b, slope.astype(BF16)))
    branch = jnp.dot(active_b, full_down, preferred_element_type=F32) + vec_f[3]
    result, norm_two_back = jax.vjp(layer_norm, normed_one + branch, vec_f[6], vec_f[7])
    result = result.astype(BF16).reshape(mine.shape)
    grad_two, grad_g2, grad_c2 = norm_two_back(cot.reshape(-1, D).astype(F32))
    grad_b2 = jnp.sum(grad_two, axis=0)
    branch_b = grad_two.astype(BF16)
    gw_down = inner(active_b, branch_b).astype(BF16)
    grad_hidden = back_mul(branch_b, full_down) * slope.astype(F32)
    grad_b1 = jnp.sum(grad_hidden, axis=0)
    hidden_b = grad_hidden.astype(BF16)
    gw_up = inner(normed_b, hidden_b).astype(BF16)
    grad_one, grad_g1, grad_c1 = norm_one_back(grad_two + back_mul(hidden_b, full_up))
    grad_bo = jnp.sum(grad_one, axis=0)
    attn_b = grad_one.astype(BF16)
    gw_out = inner(mixed, attn_b).astype(BF16)
    grad_mixed = back_mul(attn_b, full_out).astype(BF16)
    norm_rows = [grad_bo, grad_b2, grad_g1, grad_c1, grad_g2, grad_c2]
    if tuned:
        empty = jnp.zeros((2, D), F32)
        wide_vec = jnp.concatenate(
            [empty, jnp.stack(norm_rows), grad_b1.reshape(4, D), empty, empty]
        )
        by_owner = lambda g: g.reshape(4, 2, -1, g.shape[-1])
        grad_input, output, *sums = reduce_all(
            my_lengths, qkv, mixed, grad_mixed, logs, rows, full_qkv, grad_one, result,
            wide_vec, by_owner(gw_up), by_owner(gw_down), by_owner(gw_out),
        )
        at_own = (0, lax.axis_index("tab") * owned)
        sum_vec = lax.dynamic_slice(sums[4], at_own, (16, owned))[:12].T
        shares = [s.astype(F32) for s in (sums[2], sums[3], sums[0], sums[1], sum_vec)]
    else:
        grad_three, sums = attention_backward(my_lengths, qkv, mixed, logs, grad_mixed, share)
        sums = jnp.sum(sums[:, :, :2], axis=0)
        grad_bq, grad_bv = sums[:, 0].reshape(-1), sums[:, 1].reshape(-1)
        grad_qkv = jnp.concatenate([grad_three[i] for i in range(3)], axis=1)
        gw_qkv = inner(rows, grad_qkv).astype(BF16)
        grad_in = grad_one + back_mul(grad_qkv, full_qkv)
        grad_in = grad_in.astype(BF16).reshape(mine.shape)
        gw_vec = jnp.concatenate(
            [jnp.stack([grad_bq, grad_bv] + norm_rows), grad_b1.reshape(4, D)]
        )
        back = partial(lax.all_to_all, axis_name="blk", split_axis=1, concat_axis=0, tiled=True)
        grad_input, output = back(grad_in), back(result)

        def collect(grad):
            part = lax.psum_scatter(
                grad.reshape(shards, -1, grad.shape[-1]), "tab", scatter_dimension=0
            )
            return lax.psum(part.astype(BF16), "blk").astype(F32)

        shares = [collect(g) for g in (gw_qkv, gw_out, gw_up, gw_down)]
        shares.append(collect(gw_vec.T.astype(BF16)))
    grad_input = grad_input.astype(F32)
    step_float = step_count[0].astype(F32)
    results = [output, grad_input]
    for at in range(5):
        results.extend(
            adam(masters[at], shares[at], firsts[at], seconds[at], RATES[at], step_float)
        )
    return tuple(results)


def solution(mesh):
    tokens, flat, rows = P("tab", "blk", None), P("tab"), P("tab", None)
    return jax.shard_map(
        local,
        mesh=mesh,
        in_specs=(tokens, flat, tokens, P()) + (rows,) * 15,
        out_specs=(tokens, tokens) + (rows,) * 20,
        check_vma=False,
    )
```

profile of v0, /device:TPU:0, one launch (start us, length us, event | category | flops | bytes accessed | tf_op | source)
XLA Modules:
  0.0 316.9 jit_solution(12247934637478032821)
XLA Ops:
  1.4 1.2 dynamic_slice.6.len_ref
  2.6 0.7 convert_bitcast_fusion
  3.5 0.6 copy-done.16
  4.1 94.2 %gather_attend.1 = (bf16[2,512,768]{2,1,0:T(8,128)(2,1)}, bf16[2,512,768]{2,1,0:T(8,128)(2,1)}, bf16[8,96,2304]{2,1,0:T(8,128)(2,1)}, bf16[8,96,768]{2,1,0:T(8,1...) custom-call(s32[2]{0:T(128)} %dynamic_slice.6.len_ref, ...), custom_call_target="tpu_custom_call" | custom-call | tf_op jit(solution)/shard_map/gather_attend/pallas_call | solution.py:513
  98.3 1.7 convert_reduce_fusion
  100.0 1.0 convert_reduce_fusion.1
  101.1 3.8 %fusion.48 = (f32[1024]{0:T(1024)S(1)}, f32[1024,768]{1,0:T(8,128)S(1)}) fusion(f32[768]{0:T(1024)S(1)} %get-tuple-element.69, bf16[1024,768]{1,0:T(8,128)(2,1)} %get-tuple-element.42.mixed_in, bf16[768,768]{1,0:T(8,128)(2,1)} %bitcast.60, bf16[1024,768]{1,0:T(8,128)(2,1)} %bitcast.51), kind=kOutput, calls=%fused_computation.93 | convolution fusion | flops 1211104256 | bytes 7478272 | tf_op jit(solution)/shard_map/dot_general | solution.py:1148
  105.4 14.9 %fusion.4 = (bf16[1024,3072]{1,0:T(8,128)(2,1)}, bf16[1024,3072]{1,0:T(8,128)(2,1)S(1)}) fusion(f32[3072]{0:T(1024)S(1)} %add.182, bf16[768,3072]{1,0:T(8,128)(2,1)} %bitcast.54, f32[1024,768]{1,0:T(8,128)S(1)} %get-tuple-element.101, f32[768]{0:T(1024)S(1)} %get-tuple-element.67, f32[768]{0:T(1024)S(1)} %get-tuple-element.68, f32[1024]{0:T(1024)S(1)} %fusion.23, ...), kind=kOutput, calls=%fused_computation.5 | convolution fusion | flops 4873519104 | bytes 20473856 | tf_op jit(solution)/shard_map/dot_general | solution.py:1153
  120.3 5.4 %fusion.49 = (f32[1024]{0:T(1024)S(1)}, f32[1024,768]{1,0:T(8,128)S(1)}) fusion(f32[768]{0:T(1024)S(1)} %get-tuple-element.66, bf16[1024,3072]{1,0:T(8,128)(2,1)S(1)} %get-tuple-element.48, bf16[3072,768]{1,0:T(8,128)(2,1)S(1)} %bitcast.58, f32[768]{0:T(1024)S(1)} %get-tuple-element.67, f32[768]{0:T(1024)S(1)} %get-tuple-element.68, f32[1024]{0:T(1024)S(1)} %fusion.23, ...), kind=kOutput, calls=%fused_computation.94 | convolution fusion | flops 4837342208 | bytes 17323008 | tf_op jit(solution)/shard_map/dot_general | solution.py:1158
  125.7 0.5 multiply_reduce_fusion.2
  126.3 0.9 copy-done
  127.1 1.3 fusion.10
  128.4 2.6 fusion.47
  131.0 7.4 %convolution_convert_fusion = bf16[3072,768]{1,0:T(8,128)(2,1)} fusion(bf16[1024,3072]{1,0:T(8,128)(2,1)S(1)} %get-tuple-element.48, f32[1024,768]{1,0:T(8,128)S(1)} %get-tuple-element.96, f32[1024]{0:T(1024)S(1)} %negate_multiply_fusion.1), kind=kOutput, calls=%fused_computation.11 | convolution fusion | flops 4835770368 | bytes 14159872 | tf_op jit(solution)/shard_map/dot_general | solution.py:40
  138.7 10.0 %fusion.5 = (f32[3072]{0:T(1024)S(1)}, f32[1024,3072]{1,0:T(8,128)}) fusion(bf16[1024,3072]{1,0:T(8,128)(2,1)} %get-tuple-element.50, bf16[3072,768]{1,0:T(8,128)(2,1)S(1)} %bitcast.59, f32[1024,768]{1,0:T(8,128)S(1)} %get-tuple-element.96, f32[1024]{0:T(1024)S(1)} %negate_multiply_fusion.1), kind=kOutput, calls=%fused_computation.9 | convolution fusion | flops 4842845184 | bytes 26755072 | tf_op jit(solution)/shard_map/dot_general | solution.py:44
  148.7 12.6 %multiply_reduce_fusion = (f32[768]{0:T(1024)S(1)}, f32[1024]{0:T(1024)S(1)}, f32[768]{0:T(1024)S(1)}, f32[1024,768]{1,0:T(8,128)}) fusion(f32[1024,768]{1,0:T(8,128)S(1)} %get-tuple-element.101, f32[1024]{0:T(1024)S(1)} %fusion.23, f32[1024]{0:T(1024)S(1)} %broadcast_multiply_fusion.1, f32[768]{0:T(1024)S(1)} %get-tuple-element.68, ...), kind=kOutput, calls=%fused_computation.22 | convolution fusion | flops 4849136640 | bytes 33055744 | tf_op jit(solution)/shard_map/dot_general | solution.py:44
  161.3 14.0 %convolution_convert_fusion.1 = bf16[768,3072]{1,0:T(8,128)(2,1)} fusion(f32[1024,3072]{1,0:T(8,128)} %get-tuple-element.106, bf16[1024,3072]{1,0:T(8,128)(2,1)} %get-tuple-element.50, f32[1024,768]{1,0:T(8,128)S(1)} %get-tuple-element.101, f32[768]{0:T(1024)S(1)} %get-tuple-element.67, f32[768]{0:T(1024)S(1)} %get-tuple-element.68, f32[1024]{0:T(1024)S(1)} %fusion.23, ...), kind=kOutput, calls=%fused_computation.12 | convolution fusion | flops 4847566848 | bytes 26753024 | tf_op jit(solution)/shard_map/dot_general | solution.py:40
  175.3 2.8 fusion.46
  178.5 1.6 concatenate.7.vec_in
  180.1 4.0 %convolution_convert_fusion.2.do_in = bf16[1024,768]{1,0:T(8,128)(2,1)} fusion(bf16[768,768]{1,0:T(8,128)(2,1)} %bitcast.61, f32[1024,768]{1,0:T(8,128)S(1)} %get-tuple-element.92.one_in), kind=kOutput, calls=%fused_computation.36 | convolution fusion | flops 1209532416 | bytes 5898240 | tf_op jit(solution)/shard_map/dot_general | solution.py:44
  184.1 2.5 convolution_convert_fusion.3
  186.6 111.9 %attend_reduce.1 = (bf16[8,128,768]{2,1,0:T(8,128)(2,1)}, bf16[8,128,768]{2,1,0:T(8,128)(2,1)}, bf16[96,3072]{1,0:T(8,128)(2,1)}, bf16[384,768]{1,0:T(8,128)(2,1...) custom-call(s32[2]{0:T(128)} %dynamic_slice.6.len_ref, ...), custom_call_target="tpu_custom_call" | custom-call | tf_op jit(solution)/shard_map/attend_reduce/pallas_call | solution.py:1082
  298.6 1.4 fusion.31
  300.0 2.1 fusion.39
  302.1 3.7 %fusion.42 = (bf16[96,2304]{1,0:T(8,128)(2,1)}, f32[96,2304]{1,0:T(8,128)}, f32[96,2304]{1,0:T(8,128)}, f32[96,2304]{1,0:T(8,128)}) fusion(f32[96,2304]{1,0:T(8,128)S(1)} %copy-done.4, f32[]{:T(128)} %bitcast.13, f32[]{:T(128)} %bitcast.12, bf16[96,2304]{1,0:T(8,128)(2,1)} %get-tuple-element.55, f32[96,2304]{1,0:T(8,128)} %param.33, f32[96,2304]{1,0:T(8,128)} %param.28), kind=kLoop, calls=%fused_computation.89 | loop fusion | flops 3538944 | bytes 6193160 | tf_op jit(solution)/shard_map/convert_element_type | solution.py:54
  305.9 1.9 convert_element_type.108
  307.8 0.6 copy-done.8
  308.4 0.5 copy-done.9
  309.1 2.5 fusion.36
  311.6 0.9 copy-done.11
  312.7 2.6 fusion.33
  315.3 1.1 copy.44
  (66 shorter events, 1.8 us)
Async XLA Ops:
  3.5 0.6 copy-start.16
  104.8 15.4 %slice-start = ((s8[4718592]{0:T(1024)(128)(4,1)}), s8[4194304]{0:T(1024)(128)(4,1)S(1)}, s32[]{:S(2)}) async-start(s8[4718592]{0:T(1024)(128)(4,1)} %bitcast.56), calls=%async_computation | async-start | bytes 8388608
  105.4 14.9 %slice-start.1 = ((s8[4718592]{0:T(1024)(128)(4,1)}), s8[524288]{0:T(1024)(128)(4,1)S(1)}, s32[]{:S(2)}) async-start(s8[4718592]{0:T(1024)(128)(4,1)} %bitcast.56), calls=%async_computation.1 | async-start | bytes 1048576
  125.7 1.4 copy-start
  178.5 5.6 %copy-start.1 = (f32[1024,768]{1,0:T(8,128)}, f32[1024,768]{1,0:T(8,128)S(1)}, u32[]{:S(2)}) copy-start(f32[1024,768]{1,0:T(8,128)S(1)} %get-tuple-element.92.one_in) | copy-start | bytes 9437188
  180.1 4.0 %copy-start.5 = (bf16[1024,768]{1,0:T(8,128)(2,1)S(1)}, bf16[1024,768]{1,0:T(8,128)(2,1)}, u32[]{:S(2)}) copy-start(bf16[1024,768]{1,0:T(8,128)(2,1)} %get-tuple-element.42.mixed_in) | copy-start | bytes 4718596
  186.6 111.9 %copy-start.17 = (f32[96,12]{0,1:T(8,128)S(1)}, f32[96,12]{0,1:T(8,128)}, u32[]{:S(2)}) copy-start(f32[96,12]{0,1:T(8,128)} %param.27) | copy-start | bytes 13828
  186.6 112.0 %copy-start.18 = (f32[96,12]{0,1:T(8,128)S(1)}, f32[96,12]{0,1:T(8,128)}, u32[]{:S(2)}) copy-start(f32[96,12]{0,1:T(8,128)} %param.37) | copy-start | bytes 13828
  186.6 112.0 %copy-start.19 = (f32[96,12]{0,1:T(8,128)S(1)}, f32[96,12]{0,1:T(8,128)}, u32[]{:S(2)}) copy-start(f32[96,12]{0,1:T(8,128)} %param.32) | copy-start | bytes 13828
  186.6 113.4 %copy-start.12 = (f32[96,768]{1,0:T(8,128)S(1)}, f32[96,768]{1,0:T(8,128)}, u32[]{:S(2)}) copy-start(f32[96,768]{1,0:T(8,128)} %out_wide.1) | copy-start | bytes 884740
  186.6 113.4 %copy-start.15 = (f32[96,768]{1,0:T(8,128)S(1)}, f32[96,768]{1,0:T(8,128)}, u32[]{:S(2)}) copy-start(f32[96,768]{1,0:T(8,128)} %param.34) | copy-start | bytes 884740
  186.6 115.5 %copy-start.4 = (f32[96,2304]{1,0:T(8,128)S(1)}, f32[96,2304]{1,0:T(8,128)}, u32[]{:S(2)}) copy-start(f32[96,2304]{1,0:T(8,128)} %qkv_wide.1) | copy-start | bytes 2654212
  302.1 3.7 %copy-start.7 = (bf16[8,128,768]{2,1,0:T(8,128)(2,1)S(1)}, bf16[8,128,768]{2,1,0:T(8,128)(2,1)}, u32[]{:S(2)}) copy-start(bf16[8,128,768]{2,1,0:T(8,128)(2,1)} %get-tuple-element.54) | copy-start | bytes 4718596
  305.8 2.0 copy-start.2
  305.8 2.6 copy-start.8
  305.8 3.1 copy-start.9
  305.8 3.3 %copy-start.14 = (bf16[96,3072]{1,0:T(8,128)(2,1)S(1)}, bf16[96,3072]{1,0:T(8,128)(2,1)}, u32[]{:S(2)}) copy-start(bf16[96,3072]{1,0:T(8,128)(2,1)} %get-tuple-element.57) | copy-start | bytes 1769476
  309.1 2.6 copy-start.3
  309.1 2.6 copy-start.10
  309.1 3.5 %copy-start.11 = (f32[384,768]{1,0:T(8,128)S(1)}, f32[384,768]{1,0:T(8,128)}, u32[]{:S(2)}) copy-start(f32[384,768]{1,0:T(8,128)} %param.31) | copy-start | bytes 3538948
  309.1 3.6 %copy-start.13 = (bf16[384,768]{1,0:T(8,128)(2,1)S(1)}, bf16[384,768]{1,0:T(8,128)(2,1)}, u32[]{:S(2)}) copy-start(bf16[384,768]{1,0:T(8,128)(2,1)} %get-tuple-element.58) | copy-start | bytes 1769476
  312.7 2.6 copy-start.6
where the time goes:
time: 323 us; the launch traced here: 317 us
  Pallas kernels  206 us (64%)
  matrix products  74.5 us (23%)
  other arithmetic  26 us (8%)
  local copies, waits for them, and re-layouts  8.17 us (3%)
    pallas_call x1, Pallas kernels, reduce_all(): pl.pallas_call(reduce_kernel, in_specs=[pl.BlockSpec(memory_space=pltpu.S...  112 us
    pallas_call x1, Pallas kernels, gather_all(): pl.pallas_call(gather_kernel, in_specs=[pl.BlockSpec(memory_space=pltpu.S...  94.2 us
    dot_general x3, matrix products, back_mul(): lax.dot_general(left, right, (((1,), (1,)), ((), ())), preferred_element_...  26.6 us
    dot_general x3, matrix products, inner(): lax.dot_general(left, right, (((0,), (0,)), ((), ())), preferred_element_...  23.8 us
    dot_general x1, matrix products, local(): hidden = jnp.dot(normed_b, full_up, preferred_element_type=F32) + bias_up  14.9 us
    convert_element_type x5, other arithmetic, adam(): return (moment_new, square_new, master_new, master_new.astype(BF16))  12.4 us

commit v1 on v0

--- a/solution.py
+++ b/solution.py
@@ -418,9 +418,13 @@
     def project(i, carry):
         cols = pl.ds(pl.multiple_of(i * tile, tile), tile)
         weight = w_all[:, :, cols].reshape(D, tile)
-        value = jnp.dot(x_all[...].reshape(rows, D), weight, preferred_element_type=F32)
-        acts[:, cols] = (value + bias[:, cols]).astype(BF16)
-        return carry
+
+        def table(t, carry):
+            value = jnp.dot(x_all[t], weight, preferred_element_type=F32) + bias[:, cols]
+            acts[pl.ds(pl.multiple_of(t * LEN, LEN), LEN), cols] = value.astype(BF16)
+            return carry
+
+        return lax.fori_loop(0, share, table, carry)
 
     lax.fori_loop(0, 3 * D // tile, project, 0)
     puts[3]().start()
@@ -804,7 +808,7 @@
 SLABS = {
     "down_y": (1, Slab(64, D, True, 0)),
     "up_low": (0, Slab(96, D // 2, True, 1)),
-    "down": (1, Slab(64, D, False, 0, first=256)),
+    "down": (1, Slab(32, D, True, 0, first=256)),
     "up_high": (0, Slab(96, D, False, 1, first=2 * D)),
     "out": (3, Slab(96, D // 2, False, 1)),
     "v": (2, Slab(96, D // 2, False, 1, first=2 * D)),
@@ -856,9 +860,9 @@
 
 
 def reduce_kernel(
-    len_ref, acts_in, mixed_in, do_in, logs_in, x_in, w_in, one_in, y_in, vec_in,
+    len_ref, acts_in, mixed_in, do_in, logs_in, x_in, w_in, one_in, vec_in,
     up_in, down_in, out_in,
-    gin_out, y_out, up_out, down_out, qkv_out, out_out, vec_out,
+    gin_out, up_out, down_out, qkv_out, out_out, vec_out,
     acts, mixed, do, logs, x_all, w_all, one, x_turned, d, gw, gin, vec, vec_from, *rest,
 ):
     scratch, (send, recv, own) = rest[:-3], rest[-3:]
@@ -891,7 +895,7 @@
         lambda at=at, src=src, dst=dst: pltpu.make_async_copy(
             src.at[:, slot, :], dst.at[mine], own.at[N_LOADS + at]
         )
-        for at, (src, dst) in enumerate(((gin, gin_out), (y_in, y_out)))
+        for at, (src, dst) in enumerate(((gin, gin_out),))
     ]
 
     def trade(src, dst):
@@ -909,7 +913,7 @@
             )
         return made
 
-    trade_g, trade_y = trade(gin, gin_out), trade(y_in, y_out)
+    trade_g = trade(gin, gin_out)
     ways = [(z, x, y, 1 - c), (z, x, 1 - y, c), (z, 1 - x, y, c)]
     ways += [((z + j) % 4, x, y, c) for j in range(1, 4)]
     vec_sends = [
@@ -935,16 +939,12 @@
         for entry in todo:
             if entry[0] == "vec":
                 vec_task(entry[1])
-            elif entry[0] == "trade":
-                for index in trade_y:
-                    plan.start(index)
             else:
                 getattr(works[entry[0]], entry[1])()
 
     vec[0] = vec_in[...]
-    for name in ("down_y", "down", "up_low", "up_high", "out"):
+    for name in ("up_high", "up_low", "down_y", "down", "out"):
         works[name].begin()
-    kept[1]().start()
     for load in loads[:4]:
         load().wait()
 
@@ -965,15 +965,27 @@
     do_tasks(AFTER["attention"])
     loads[4]().wait()
     rows = share * LEN
-    x_turned[...] = x_all[...].T
+
+    def turn(i, carry):
+        part = pl.ds(pl.multiple_of(i * 128, 128), 128)
+        x_turned[:, part] = x_all[part, :].T
+        return carry
+
+    lax.fori_loop(0, rows // 128, turn, 0)
     tile = 256
     tiles = D // tile
 
     def grad_tile(i, carry):
         at = (2 - i // tiles) * tiles + i % tiles
         cols = pl.ds(pl.multiple_of(at * tile, tile), tile)
-        value = jnp.dot(x_turned[...], d[:, cols], preferred_element_type=F32)
-        gw[:, :, :, cols] = value.astype(BF16).reshape(4, 2, D // 8, tile)
+
+        def owners(t, carry):
+            left = x_turned[pl.ds(pl.multiple_of(t * (D // 2), D // 2), D // 2), :]
+            value = jnp.dot(left, d[:, cols], preferred_element_type=F32)
+            gw[pl.ds(t * 2, 2), :, :, cols] = value.astype(BF16).reshape(2, 2, D // 8, tile)
+            return carry
+
+        lax.fori_loop(0, 2, owners, 0)
         for part, name in enumerate(("v", "k", "q")):
 
             @pl.when(i == part * tiles + tiles - 1)
@@ -989,8 +1001,14 @@
 
     def token_tile(i, carry):
         cols = pl.ds(pl.multiple_of(i * tile, tile), tile)
-        value = back_mul(d[...], w_all[cols, :]) + one[:, cols]
-        gin[:, :, cols] = value.astype(BF16).reshape(share, LEN, tile)
+
+        def table(t, carry):
+            at = pl.ds(pl.multiple_of(t * LEN, LEN), LEN)
+            value = back_mul(d[at, :], w_all[cols, :]) + one[at, cols]
+            gin[t, :, cols] = value.astype(BF16)
+            return carry
+
+        lax.fori_loop(0, share, table, 0)
         for when in range(D // tile):
 
             @pl.when(i == when)
@@ -1007,57 +1025,53 @@
     vec_end()
     for work in works.values():
         work.end()
-    for index in trade_g + trade_y:
+    for index in trade_g:
         plan.arrived(index)
     for work in works.values():
         work.finish_sends()
-    for index in trade_g + trade_y + vec_sends:
+    for index in trade_g + vec_sends:
         plan.build(index).wait_send()
     for made in kept:
         made().wait()
 
 
 DURING = {
-    0: [("down_y", "after_core")],
-    1: [("down", "after_core"), ("up_low", "after_core")],
-    2: [("up_high", "after_core")],
-    3: [("out", "after_core"), ("trade",)],
-    7: [("down", "after_x")],
-    9: [("down_y", "after_y")],
-    11: [("up_high", "after_x")],
+    0: [("up_high", "after_core")],
+    1: [("up_low", "after_core")],
+    2: [("down_y", "after_core")],
+    3: [("down", "after_core")],
+    4: [("out", "after_core")],
+    7: [("up_low", "after_y")],
+    8: [("up_high", "after_x")],
+    11: [("out", "after_x")],
 }
 AFTER = {
-    "attention": [("vec", 0), ("down", "after_a")],
-    "v": [("vec", 1), ("up_low", "after_y")],
-    "k": [("v", "after_core"), ("vec", 2)],
-    "q": [("k", "after_core"), ("vec", 3), ("out", "after_x"), ("down", "after_b")],
-    0: [("q", "after_core"), ("up_high", "after_a")],
-    1: [("down", "after_z"), ("down_y", "after_x")],
-    2: [("up_high", "after_b")],
+    "attention": [("vec", 0), ("up_high", "after_a"), ("up_low", "after_x")],
+    "v": [("vec", 1)],
+    "k": [("v", "after_core"), ("vec", 2), ("down_y", "after_y"), ("out", "after_a")],
+    "q": [("k", "after_core"), ("vec", 3), ("up_high", "after_b"), ("up_low", "after_a")],
+    0: [("q", "after_core"), ("out", "after_b")],
+    1: [("down", "after_y"), ("up_high", "after_z")],
+    2: [("down_y", "after_x"), ("up_low", "after_b"), ("out", "after_z")],
     "end": [
-        ("out", "after_a"),
-        ("up_low", "after_x"),
+        ("v", "after_x"),
         ("down_y", "after_a"),
-        ("out", "after_b"),
-        ("up_high", "after_z"),
+        ("up_low", "after_z"),
+        ("k", "after_x"),
+        ("v", "after_a"),
         ("down_y", "after_b"),
-        ("up_low", "after_a"),
-        ("v", "after_x"),
-        ("out", "after_z"),
+        ("q", "after_x"),
+        ("k", "after_a"),
+        ("v", "after_b"),
         ("down_y", "after_z"),
-        ("up_low", "after_b"),
-        ("v", "after_a"),
-        ("k", "after_x"),
-        ("up_low", "after_z"),
-        ("v", "after_b"),
-        ("k", "after_a"),
-        ("q", "after_x"),
+        ("down", "after_x"),
         ("v", "after_z"),
+        ("q", "after_a"),
         ("k", "after_b"),
-        ("q", "after_a"),
+        ("down", "after_a"),
         ("k", "after_z"),
         ("q", "after_b"),
-        ("down", "after_final"),
+        ("down", "after_b"),
         ("up_high", "after_final"),
         ("out", "after_final"),
         ("down_y", "after_final"),
@@ -1066,12 +1080,14 @@
         ("v", "after_final"),
         ("k", "after_final"),
         ("q", "after_final"),
+        ("down", "after_z"),
+        ("down", "after_final"),
     ],
 }
 
 
-def reduce_all(lengths, acts, mixed, do, logs, rows, whole, one, result, vec, up, down, out):
-    share, length = result.shape[:2]
+def reduce_all(lengths, acts, mixed, do, logs, rows, whole, one, vec, up, down, out):
+    share, length = acts.shape[0] // LEN, LEN
     vmem = pl.BlockSpec(memory_space=pltpu.VMEM)
     hbm = pl.BlockSpec(memory_space=pl.ANY)
     shape = lambda a: jax.ShapeDtypeStruct(a.shape[2:], a.dtype)
@@ -1081,10 +1097,10 @@
     like = lambda a: pltpu.VMEM(a.shape, a.dtype)
     return pl.pallas_call(
         reduce_kernel,
-        in_specs=[pl.BlockSpec(memory_space=pltpu.SMEM)] + [hbm] * 7 + [vmem] * 2 + [hbm] * 3,
-        out_specs=[hbm] * 6 + [vmem],
+        in_specs=[pl.BlockSpec(memory_space=pltpu.SMEM)] + [hbm] * 7 + [vmem] + [hbm] * 3,
+        out_specs=[hbm] * 5 + [vmem],
         out_shape=[
-            back, back, shape(up), shape(down),
+            back, shape(up), shape(down),
             jax.ShapeDtypeStruct((D // 8, 3 * D), BF16),
             shape(out),
             jax.ShapeDtypeStruct((16, D), F32),
@@ -1108,7 +1124,19 @@
             collective_id=1, has_side_effects=True, vmem_limit_bytes=VMEM_ALL
         ),
         name="attend_reduce",
-    )(lengths, acts, mixed, do, logs, rows, whole, one, result, vec, up, down, out)
+    )(lengths, acts, mixed, do, logs, rows, whole, one, vec, up, down, out)
+
+
+def send_back(result, share):
+    blk, span = lax.axis_index("blk"), result.shape[1] // 4
+    piece = lambda at: lax.dynamic_slice_in_dim(result, at * span, span, axis=1)
+    output = jnp.zeros((4 * share, span, D), BF16)
+    output = lax.dynamic_update_slice_in_dim(output, piece(blk), blk * share, axis=0)
+    for k in (1, 2, 3):
+        other = blk ^ k
+        got = lax.ppermute(piece(other), "blk", [(b, b ^ k) for b in range(4)])
+        output = lax.dynamic_update_slice_in_dim(output, got, other * share, axis=0)
+    return output
 
 
 def local(*args):
@@ -1178,8 +1206,9 @@
             [empty, jnp.stack(norm_rows), grad_b1.reshape(4, D), empty, empty]
         )
         by_owner = lambda g: g.reshape(4, 2, -1, g.shape[-1])
-        grad_input, output, *sums = reduce_all(
-            my_lengths, qkv, mixed, grad_mixed, logs, rows, full_qkv, grad_one, result,
+        output = send_back(result, share)
+        grad_input, *sums = reduce_all(
+            my_lengths, qkv, mixed, grad_mixed, logs, rows, full_qkv, grad_one,
             wide_vec, by_owner(gw_up), by_owner(gw_down), by_owner(gw_out),
         )
         at_own = (0, lax.axis_index("tab") * owned)

time: 323 us -> 313 us (0.969); the launches traced: 317 us -> 313 us
  Pallas kernels: 206 us -> 200 us
  local copies, waits for them, and re-layouts: 8.17 us -> 11.8 us
    pallas_call x1, Pallas kernels: 112 us -> 104 us  [reduce_all(): pl.pallas_call(reduce_kernel, in_specs=[pl.BlockSpec(memory_space=pltpu.S...]
  transfers between devices with their start and end apart: 0 -> 3, of which waited for: 0 -> 0; matrix products, arithmetic and copies ran while one was open for 0% -> 22% of each run, Pallas kernels for 0% -> 33%
where the time goes in v1:
time: 313 us
  Pallas kernels  200 us (64%)
  matrix products  74.1 us (24%)
  other arithmetic  23.3 us (7%)
  local copies, waits for them, and re-layouts  11.8 us (4%)
    pallas_call x1, Pallas kernels, reduce_all(): pl.pallas_call(reduce_kernel, in_specs=[pl.BlockSpec(memory_space=pltpu.S...  104 us
    pallas_call x1, Pallas kernels, gather_all(): pl.pallas_call(gather_kernel, in_specs=[pl.BlockSpec(memory_space=pltpu.S...  95.7 us
    dot_general x3, matrix products, inner(): lax.dot_general(left, right, (((0,), (0,)), ((), ())), preferred_element_...  26.9 us
    dot_general x3, matrix products, back_mul(): lax.dot_general(left, right, (((1,), (1,)), ((), ())), preferred_element_...  24.2 us
    dot_general x1, matrix products, local(): hidden = jnp.dot(normed_b, full_up, preferred_element_type=F32) + bias_up  13.7 us
    convert_element_type x5, other arithmetic, adam(): return (moment_new, square_new, master_new, master_new.astype(BF16))  11.4 us
  transfers between devices with their start and end apart: 3, of which 0 were waited for; matrix products, arithmetic and copies ran while one was open for 22% of the time, Pallas kernels for 33%

profile of v1, /device:TPU:0, one launch (start us, length us, event | category | flops | bytes accessed | tf_op | source)
XLA Modules:
  0.0 312.9 jit_solution(11692402948907298008)
XLA Ops:
  1.4 1.2 dynamic_slice.18.len_ref
  3.4 95.7 %gather_attend.1 = (bf16[2,512,768]{2,1,0:T(8,128)(2,1)}, bf16[2,512,768]{2,1,0:T(8,128)(2,1)}, bf16[8,96,2304]{2,1,0:T(8,128)(2,1)}, bf16[8,96,768]{2,1,0:T(8,1...) custom-call(s32[2]{0:T(128)} %dynamic_slice.18.len_ref, ...), custom_call_target="tpu_custom_call" | custom-call | tf_op jit(solution)/shard_map/gather_attend/pallas_call | solution.py:517
  99.1 1.0 convert_reduce_fusion.1
  100.2 3.9 %fusion.48 = (f32[1024]{0:T(1024)S(1)}, f32[1024,768]{1,0:T(8,128)S(1)}) fusion(f32[768]{0:T(1024)S(1)} %get-tuple-element.68, bf16[1024,768]{1,0:T(8,128)(2,1)} %get-tuple-element.41.mixed_in, bf16[768,768]{1,0:T(8,128)(2,1)} %bitcast.64, bf16[1024,768]{1,0:T(8,128)(2,1)} %bitcast.51), kind=kOutput, calls=%fused_computation.100 | convolution fusion | flops 1211104256 | bytes 7478272 | tf_op jit(solution)/shard_map/dot_general | solution.py:1176
  104.7 13.7 %fusion.4 = (bf16[1024,3072]{1,0:T(8,128)(2,1)}, bf16[1024,3072]{1,0:T(8,128)(2,1)S(1)}) fusion(f32[3072]{0:T(1024)S(1)} %add.204, bf16[768,3072]{1,0:T(8,128)(2,1)S(1)} %bitcast.57, f32[1024,768]{1,0:T(8,128)S(1)} %get-tuple-element.103, f32[768]{0:T(1024)S(1)} %get-tuple-element.66, f32[768]{0:T(1024)S(1)} %get-tuple-element.67, f32[1024]{0:T(1024)S(1)} %fusion.23, ...), kind=kOutput, calls=%fused_computation.5 | convolution fusion | flops 4873519104 | bytes 20473856 | tf_op jit(solution)/shard_map/dot_general | solution.py:1181
  118.4 5.4 %fusion.49 = (f32[1024]{0:T(1024)S(1)}, f32[1024,768]{1,0:T(8,128)S(1)}) fusion(f32[768]{0:T(1024)S(1)} %get-tuple-element.65, bf16[1024,3072]{1,0:T(8,128)(2,1)S(1)} %get-tuple-element.45, bf16[3072,768]{1,0:T(8,128)(2,1)S(1)} %bitcast.60, f32[768]{0:T(1024)S(1)} %get-tuple-element.66, f32[768]{0:T(1024)S(1)} %get-tuple-element.67, f32[1024]{0:T(1024)S(1)} %fusion.23, ...), kind=kOutput, calls=%fused_computation.101 | convolution fusion | flops 4837342208 | bytes 17323008 | tf_op jit(solution)/shard_map/dot_general | solution.py:1186
  124.4 0.9 copy-done
  125.3 1.7 fusion.10
  127.1 3.0 fusion.47
  130.2 1.0 constant_dynamic-slice_fusion
  131.2 1.0 collective-permute-start.2
  132.3 1.1 collective-permute-start.1
  133.6 10.4 %convolution_convert_fusion = bf16[3072,768]{1,0:T(8,128)(2,1)} fusion(bf16[1024,3072]{1,0:T(8,128)(2,1)} %copy-done.30, f32[1024,768]{1,0:T(8,128)S(1)} %get-tuple-element.94, f32[1024]{0:T(1024)S(1)} %negate_multiply_fusion.1), kind=kOutput, calls=%fused_computation.11 | convolution fusion | flops 4835770368 | bytes 14159872 | tf_op jit(solution)/shard_map/dot_general | solution.py:40
  144.3 10.2 %fusion.5 = (f32[3072]{0:T(1024)S(1)}, f32[1024,3072]{1,0:T(8,128)}) fusion(bf16[1024,3072]{1,0:T(8,128)(2,1)} %get-tuple-element.49, bf16[3072,768]{1,0:T(8,128)(2,1)S(1)} %bitcast.63, f32[1024,768]{1,0:T(8,128)S(1)} %get-tuple-element.94, f32[1024]{0:T(1024)S(1)} %negate_multiply_fusion.1), kind=kOutput, calls=%fused_computation.9 | convolution fusion | flops 4842845184 | bytes 26755072 | tf_op jit(solution)/shard_map/dot_general | solution.py:44
  154.5 11.4 %multiply_reduce_fusion = (f32[768]{0:T(1024)S(1)}, f32[1024]{0:T(1024)S(1)}, f32[768]{0:T(1024)S(1)}, f32[1024,768]{1,0:T(8,128)S(1)}) fusion(f32[1024,768]{1,0:T(8,128)S(1)} %copy-done.3, f32[1024]{0:T(1024)S(1)} %fusion.23, f32[1024]{0:T(1024)S(1)} %broadcast_multiply_fusion.1, f32[768]{0:T(1024)S(1)} %get-tuple-element.67, ...), kind=kOutput, calls=%fused_computation.22 | convolution fusion | flops 4849136640 | bytes 33055744 | tf_op jit(solution)/shard_map/dot_general | solution.py:44
  165.9 14.0 %convolution_convert_fusion.1 = bf16[768,3072]{1,0:T(8,128)(2,1)} fusion(f32[1024,3072]{1,0:T(8,128)} %get-tuple-element.108, bf16[1024,3072]{1,0:T(8,128)(2,1)} %get-tuple-element.49, f32[1024,768]{1,0:T(8,128)S(1)} %copy-done.3, f32[768]{0:T(1024)S(1)} %copy-done.28, f32[768]{0:T(1024)S(1)} %get-tuple-element.67, f32[1024]{0:T(1024)S(1)} %fusion.23, ...), kind=kOutput, calls=%fused_computation.12 | convolution fusion | flops 4847566848 | bytes 26753024 | tf_op jit(solution)/shard_map/dot_general | solution.py:40
  180.0 1.7 fusion.46
  182.0 0.9 copy-done.29
  182.9 2.6 convolution_convert_fusion.2.do_in
  185.5 2.5 convolution_convert_fusion.3
  188.9 1.3 concatenate.7.vec_in
  190.2 103.9 %attend_reduce.1 = (bf16[8,128,768]{2,1,0:T(8,128)(2,1)}, bf16[96,3072]{1,0:T(8,128)(2,1)}, bf16[384,768]{1,0:T(8,128)(2,1)}, bf16[96,2304]{1,0:T(8,128)(2,1)}, ...) custom-call(s32[2]{0:T(128)} %dynamic_slice.18.len_ref, bf16[1024,2304]{1,0:T(8,128)(2,1)} %get-tuple-element.47.acts_in, ...), custom_call_target="tpu_custom_call" | custom-call | tf_op jit(solution)/shard_map/attend_reduce/pallas_call | solution.py:1098
  294.2 3.8 %fusion.42 = (bf16[96,2304]{1,0:T(8,128)(2,1)}, f32[96,2304]{1,0:T(8,128)}, f32[96,2304]{1,0:T(8,128)}, f32[96,2304]{1,0:T(8,128)}) fusion(f32[96,2304]{1,0:T(8,128)S(1)} %copy-done.7, f32[]{:T(128)} %bitcast.13, f32[]{:T(128)} %bitcast.12, bf16[96,2304]{1,0:T(8,128)(2,1)} %get-tuple-element.53, f32[96,2304]{1,0:T(8,128)} %param.33, f32[96,2304]{1,0:T(8,128)} %param.28), kind=kLoop, calls=%fused_computation.96 | loop fusion | flops 3538944 | bytes 6193160 | tf_op jit(solution)/shard_map/convert_element_type | solution.py:54
  298.0 2.5 fusion.36
  301.6 2.6 fusion.33
  304.2 1.1 fusion.39
  305.3 1.9 convert_element_type.108
  307.2 1.4 fusion.31
  308.7 1.0 constant_dynamic-update-slice_fusion.2
  309.7 1.0 constant_dynamic-update-slice_fusion.1
  310.7 1.0 constant_dynamic-update-slice_fusion
  311.8 1.1 copy-done.10
  (108 shorter events, 4.8 us)
Async XLA Ops:
  100.1 18.3 %copy-start.27 = (f32[768]{0:T(1024)}, f32[768]{0:T(1024)S(1)}, u32[]{:S(2)}) copy-start(f32[768]{0:T(1024)S(1)} %get-tuple-element.66) | copy-start | bytes 9220
  100.2 4.5 %slice-start = ((s8[4718592]{0:T(1024)(128)(4,1)}), s8[4194304]{0:T(1024)(128)(4,1)S(1)}, s32[]{:S(2)}) async-start(s8[4718592]{0:T(1024)(128)(4,1)} %bitcast.55), calls=%async_computation | async-start | bytes 8388608
  100.2 4.5 %slice-start.1 = ((s8[4718592]{0:T(1024)(128)(4,1)}), s8[524288]{0:T(1024)(128)(4,1)S(1)}, s32[]{:S(2)}) async-start(s8[4718592]{0:T(1024)(128)(4,1)} %bitcast.55), calls=%async_computation.1 | async-start | bytes 1048576
  104.1 14.3 %copy-start.2 = (f32[1024,768]{1,0:T(8,128)}, f32[1024,768]{1,0:T(8,128)S(1)}, u32[]{:S(2)}) copy-start(f32[1024,768]{1,0:T(8,128)S(1)} %get-tuple-element.103) | copy-start | bytes 9437188
  104.1 14.3 %slice-start.2 = ((s8[4718592]{0:T(1024)(128)(4,1)}), s8[4194304]{0:T(1024)(128)(4,1)S(1)}, s32[]{:S(2)}) async-start(s8[4718592]{0:T(1024)(128)(4,1)} %bitcast.58), calls=%async_computation.2 | async-start | bytes 8388608
  104.7 13.7 %slice-start.3 = ((s8[4718592]{0:T(1024)(128)(4,1)}), s8[524288]{0:T(1024)(128)(4,1)S(1)}, s32[]{:S(2)}) async-start(s8[4718592]{0:T(1024)(128)(4,1)} %bitcast.58), calls=%async_computation.3 | async-start | bytes 1048576
  118.4 5.5 %copy-start.30 = (bf16[1024,3072]{1,0:T(8,128)(2,1)}, bf16[1024,3072]{1,0:T(8,128)(2,1)S(1)}, u32[]{:S(2)}) copy-start(bf16[1024,3072]{1,0:T(8,128)(2,1)S(1)} %get-tuple-element.45) | copy-start | bytes 18874372
  130.0 3.3 %copy-start.1 = (bf16[2,512,768]{2,1,0:T(8,128)(2,1)S(1)}, bf16[2,512,768]{2,1,0:T(8,128)(2,1)}, u32[]{:S(2)}) copy-start(bf16[2,512,768]{2,1,0:T(8,128)(2,1)} %get-tuple-element.48) | copy-start | bytes 4718596
  130.2 14.1 %slice-start.4 = ((s8[4718592]{0:T(1024)(128)(4,1)}), s8[4194304]{0:T(1024)(128)(4,1)S(1)}, s32[]{:S(2)}) async-start(s8[4718592]{0:T(1024)(128)(4,1)} %bitcast.61), calls=%async_computation.4 | async-start | bytes 8388608
  131.2 179.5 %collective-permute-start.2 = (bf16[2,128,768]{2,1,0:T(8,128)(2,1)S(1)}, bf16[2,128,768]{2,1,0:T(8,128)(2,1)}, u32[]{:S(2)}, u32[]{:S(2)}) collective-permute-start(bf16[2,128,768]{2,1,0:T(8,128)(2,1)S(1)} %get-tuple-element.98), channel_id=1, source_target_pairs={{0,3},{1,2},{2,1},{3,0},{4,7},{5,6},{6,5},{7,4},{8,11},{9,10},{10,... | collective-permute-start | bytes 1179656 | tf_op jit(solution)/shard_map/ppermute | solution.py:1137
  132.3 177.4 %collective-permute-start.1 = (bf16[2,128,768]{2,1,0:T(8,128)(2,1)}, bf16[2,128,768]{2,1,0:T(8,128)(2,1)}, u32[]{:S(2)}, u32[]{:S(2)}) collective-permute-start(bf16[2,128,768]{2,1,0:T(8,128)(2,1)} %get-tuple-element.99), channel_id=1, source_target_pairs={{0,2},{1,3},{2,0},{3,1},{4,6},{5,7},{6,4},{7,5},{8,10},{9,11},{10,... | collective-permute-start | bytes 1179656 | tf_op jit(solution)/shard_map/ppermute | solution.py:1137
  133.3 175.3 %collective-permute-start = (bf16[2,128,768]{2,1,0:T(8,128)(2,1)}, bf16[2,128,768]{2,1,0:T(8,128)(2,1)}, u32[]{:S(2)}, u32[]{:S(2)}) collective-permute-start(bf16[2,128,768]{2,1,0:T(8,128)(2,1)} %get-tuple-element.100), channel_id=1, source_target_pairs={{0,1},{1,0},{2,3},{3,2},{4,5},{5,4},{6,7},{7,6},{8,9},{9,8},{10,11... | collective-permute-start | bytes 1179656 | tf_op jit(solution)/shard_map/ppermute | solution.py:1137
  133.6 10.7 %slice-start.5 = ((s8[4718592]{0:T(1024)(128)(4,1)}), s8[524288]{0:T(1024)(128)(4,1)S(1)}, s32[]{:S(2)}) async-start(s8[4718592]{0:T(1024)(128)(4,1)} %bitcast.61), calls=%async_computation.5 | async-start | bytes 1048576
  144.3 10.2 %copy-start.3 = (f32[1024,768]{1,0:T(8,128)S(1)}, f32[1024,768]{1,0:T(8,128)}, u32[]{:S(2)}) copy-start(f32[1024,768]{1,0:T(8,128)} %copy-done.2) | copy-start | bytes 9437188
  154.5 11.4 %copy-start.28 = (f32[768]{0:T(1024)S(1)}, f32[768]{0:T(1024)}, u32[]{:S(2)}) copy-start(f32[768]{0:T(1024)} %copy-done.27) | copy-start | bytes 9220
  182.0 3.5 %copy-start.4 = (f32[1024,768]{1,0:T(8,128)}, f32[1024,768]{1,0:T(8,128)S(1)}, u32[]{:S(2)}) copy-start(f32[1024,768]{1,0:T(8,128)S(1)} %get-tuple-element.90.one_in) | copy-start | bytes 9437188
  182.9 2.6 copy-start.12
  185.5 3.2 %copy-start.25 = (f32[768]{0:T(1024)S(1)}, f32[768]{0:T(1024)}, u32[]{:S(2)}) copy-start(f32[768]{0:T(1024)} %get-tuple-element.60) | copy-start | bytes 9220
  190.2 104.0 %copy-start.7 = (f32[96,2304]{1,0:T(8,128)S(1)}, f32[96,2304]{1,0:T(8,128)}, u32[]{:S(2)}) copy-start(f32[96,2304]{1,0:T(8,128)} %qkv_wide.1) | copy-start | bytes 2654212
  294.1 3.8 %copy-start.5 = (f32[96,3072]{1,0:T(8,128)S(1)}, f32[96,3072]{1,0:T(8,128)}, u32[]{:S(2)}) copy-start(f32[96,3072]{1,0:T(8,128)} %up_wide.1) | copy-start | bytes 3538948
  294.1 3.8 %copy-start.13 = (f32[96,3072]{1,0:T(8,128)S(1)}, f32[96,3072]{1,0:T(8,128)}, u32[]{:S(2)}) copy-start(f32[96,3072]{1,0:T(8,128)} %param.35) | copy-start | bytes 3538948
  294.1 3.8 %copy-start.14 = (f32[96,3072]{1,0:T(8,128)S(1)}, f32[96,3072]{1,0:T(8,128)}, u32[]{:S(2)}) copy-start(f32[96,3072]{1,0:T(8,128)} %param.30) | copy-start | bytes 3538948
  294.1 3.8 %copy-start.19 = (bf16[96,3072]{1,0:T(8,128)(2,1)S(1)}, bf16[96,3072]{1,0:T(8,128)(2,1)}, u32[]{:S(2)}) copy-start(bf16[96,3072]{1,0:T(8,128)(2,1)} %get-tuple-element.55) | copy-start | bytes 1769476
  297.9 2.6 copy-start.6
  298.0 3.5 %copy-start.16 = (f32[384,768]{1,0:T(8,128)S(1)}, f32[384,768]{1,0:T(8,128)}, u32[]{:S(2)}) copy-start(f32[384,768]{1,0:T(8,128)} %param.31) | copy-start | bytes 3538948
  298.0 3.6 %copy-start.18 = (bf16[384,768]{1,0:T(8,128)(2,1)S(1)}, bf16[384,768]{1,0:T(8,128)(2,1)}, u32[]{:S(2)}) copy-start(bf16[384,768]{1,0:T(8,128)(2,1)} %get-tuple-element.56) | copy-start | bytes 1769476
  301.6 2.6 copy-start.21
  301.6 2.6 copy-start.22
  301.6 3.7 %copy-start.11 = (bf16[8,128,768]{2,1,0:T(8,128)(2,1)S(1)}, bf16[8,128,768]{2,1,0:T(8,128)(2,1)}, u32[]{:S(2)}) copy-start(bf16[8,128,768]{2,1,0:T(8,128)(2,1)} %get-tuple-element.52) | copy-start | bytes 4718596
  304.1 3.1 copy-start.24
  304.2 3.1 copy-start.26
  304.2 4.5 %copy-start.9 = (bf16[8,128,768]{2,1,0:T(8,128)(2,1)S(1)}, bf16[8,128,768]{2,1,0:T(8,128)(2,1)}, u32[]{:S(2)}) copy-start(bf16[8,128,768]{2,1,0:T(8,128)(2,1)} %copy-done.8) | copy-start | bytes 4718596
  (8 other events, 14.6 us)
